TPU v7x, 32 devices: a whole 2x2x4 slice. The times are simulated.
32 devices in a mesh: groups: 2 (over y), space: 4 (over z), tm: 2 (over x), chan: 2 (over core).
Axes of the slice: x: 2, y: 2, z: 4, core: 2. Of those that a mesh axis runs over, the one named last changes fastest.
Arguments:
- hidden_states: bfloat16 [8, 4, 64, 512], P(('groups', 'tm'), 'space', None, 'chan'), parts along dimension 0, may hold values from -25 to 25
- first_gain: float32 [512], P('chan'), may hold values from 0.1 to 1.9
- second_gain: float32 [512], P('chan'), may hold values from 0.1 to 1.9
- query_weight: bfloat16 [512, 512], replicated, may hold values from -0.4861359 to 0.4861359
- key_weight: bfloat16 [512, 512], replicated, may hold values from -0.4861359 to 0.4861359
- value_weight: bfloat16 [512, 512], replicated, may hold values from -0.25 to 0.25
- out_weight: bfloat16 [512, 512], replicated, may hold values from -0.25 to 0.25
- conv_kernel: bfloat16 [3, 3, 3, 512, 512], P(None, None, None, 'tm', 'chan'), may hold values from -0.0546875 to 0.0546875
Outputs:
- attended: bfloat16 [8, 4, 64, 512], P(('groups', 'tm'), 'space', None, 'chan'), parts along dimension 0
- convolved: bfloat16 [8, 4, 64, 512], P(('groups', 'tm'), 'space', None, 'chan'), parts along dimension 0
There are 2 independent parts, one for each index of `groups`. A program takes and returns all parts, laid end to end along the dimension named above; an argument that names none is the same for every part. Nothing has to cross between parts.
All inputs are finite; a program needn't handle non-finite values.
Results may differ from a plain program's by a relative error of at most 0.012.
The roundings to bfloat16 on the way count: a program that leaves them out, or rounds other values in their place, can miss the bound.
Values may be sent and summed in bfloat16 or wider, within the bound.
A program may use at most 64 MiB of HBM per device.

v0:
```python
import jax
import jax.numpy as jnp
from jax import lax
from jax.sharding import PartitionSpec as P

D = 512
NGROUP = 32
EPSILON = 1e-06


def shifted_2(x, axis, by):
    peers = lax.axis_size(axis)
    pairs = [(i, i + by) for i in range(peers) if 0 <= i + by < peers]
    return lax.ppermute(x, axis, pairs)


def padded_2(cells, sides, width):
    for axis, dim in sides:
        count = lax.axis_size(axis)
        ends = count - 1
        head = lax.slice_in_dim(cells, 0, width, axis=dim)
        tail = lax.slice_in_dim(cells, cells.shape[dim] - width, cells.shape[dim], axis=dim)
        cells = jnp.concatenate(
            [
                lax.ppermute(tail, axis, [(i, (i + 1) % count) for i in range(ends)]),
                cells,
                lax.ppermute(head, axis, [((i + 1) % count, i) for i in range(ends)]),
            ],
            axis=dim,
        )
    return cells


def normalize(source, gain_vector):
    channels = source.shape[3]
    group_width = D // NGROUP
    grouped = source.reshape(-1, channels // group_width, group_width)
    population = grouped.shape[0] * group_width * lax.axis_size("space") * lax.axis_size("tm")
    group_sums, group_squares = lax.psum(
        (jnp.sum(grouped, axis=(0, 2)), jnp.sum(grouped * grouped, axis=(0, 2))), ("space", "tm")
    )
    centre = group_sums / population
    spread = jnp.maximum(group_squares / population - centre * centre, 0.0)
    shifted = grouped - centre[None, :, None]
    scaled = shifted * lax.rsqrt(spread + EPSILON)[None, :, None]
    return scaled.reshape(source.shape) * gain_vector


def attend(normed, query_weight, key_weight, value_weight, out_weight):
    frame_count, row_count, col_count, channels = normed.shape
    token_count = frame_count * row_count * col_count
    tokens = normed.reshape(token_count, channels)
    halves = lax.all_to_all(tokens, "chan", split_axis=0, concat_axis=1, tiled=True)
    half_rows = halves.shape[0]
    queries = jnp.dot(halves, query_weight, preferred_element_type=jnp.float32).astype(jnp.bfloat16)
    keyed = jnp.dot(halves, key_weight, preferred_element_type=jnp.float32).astype(jnp.bfloat16)
    valued = jnp.dot(halves, value_weight, preferred_element_type=jnp.float32).astype(jnp.bfloat16)
    score_scale = D ** (-0.5)
    running_max = jnp.full((half_rows,), -1e30, jnp.float32)
    key_piece = lax.all_gather(keyed, "space", axis=0, tiled=True)
    value_piece = lax.all_gather(valued, "space", axis=0, tiled=True)
    scores = jnp.dot(queries, key_piece.T, preferred_element_type=jnp.float32) * score_scale
    newest_max = jnp.maximum(running_max, jnp.max(scores, axis=1))
    weights = jnp.exp(scores - newest_max[:, None])
    running_sum = jnp.sum(weights, axis=1)
    accumulated = jnp.dot(
        weights.astype(jnp.bfloat16), value_piece, preferred_element_type=jnp.float32
    )
    mixed = (accumulated / running_sum[:, None]).astype(jnp.bfloat16)
    projected = jnp.dot(mixed, out_weight, preferred_element_type=jnp.float32).astype(jnp.bfloat16)
    returned = lax.all_to_all(projected, "chan", split_axis=1, concat_axis=0, tiled=True)
    return returned.reshape(frame_count, row_count, col_count, channels)


def join_channels(activated):
    return lax.all_gather(activated, "chan", axis=3, tiled=True)


def extend(frames_in):
    earlier = shifted_2(frames_in, "tm", 1)
    timed = jnp.concatenate([earlier, frames_in], axis=0)
    rimmed = padded_2(timed, (("space", 1),), 1)
    return jnp.pad(rimmed, ((0, 0), (0, 0), (1, 1), (0, 0)))


def convolve(activated, conv_kernel):
    frame_count, row_count, col_count = (activated.shape[0], activated.shape[1], activated.shape[2])
    padded = extend(join_channels(activated))
    out_width = conv_kernel.shape[4]
    initial = jnp.zeros((frame_count * row_count * col_count, out_width), jnp.float32)
    running_total = initial
    piece = lax.all_gather(conv_kernel, "tm", axis=3, tiled=True)
    for time_tap in range(3):
        for row_tap in range(3):
            for col_tap in range(3):
                window = padded[
                    time_tap : time_tap + frame_count,
                    row_tap : row_tap + row_count,
                    col_tap : col_tap + col_count,
                ]
                window = window.reshape(frame_count * row_count * col_count, piece.shape[3])
                running_total = running_total + jnp.dot(
                    window, piece[time_tap, row_tap, col_tap], preferred_element_type=jnp.float32
                )
    return running_total.reshape(frame_count, row_count, col_count, out_width).astype(jnp.bfloat16)


def on_device(
    hidden_states,
    first_gain,
    second_gain,
    query_weight,
    key_weight,
    value_weight,
    out_weight,
    conv_kernel,
):
    source = hidden_states.astype(jnp.float32)
    normed = normalize(source, first_gain).astype(jnp.bfloat16)
    attended = attend(normed, query_weight, key_weight, value_weight, out_weight)
    resid = source + attended.astype(jnp.float32)
    activated = jax.nn.silu(normalize(resid, second_gain)).astype(jnp.bfloat16)
    convolved = convolve(activated, conv_kernel)
    return (attended, convolved)


def solution(mesh):
    placed = (
        P(("groups", "tm"), "space", None, "chan"),
        P("chan"),
        P("chan"),
        P(),
        P(),
        P(),
        P(),
        P(None, None, None, "tm", "chan"),
    )
    return jax.shard_map(
        on_device,
        mesh=mesh,
        in_specs=placed,
        out_specs=(
            P(("groups", "tm"), "space", None, "chan"),
            P(("groups", "tm"), "space", None, "chan"),
        ),
        check_vma=False,
    )
```

profile of v0, /device:TPU:0, one launch (start us, length us, event | category | flops | bytes accessed | tf_op | source)
XLA Modules:
  0.0 143.7 jit_solution(14035605134556565551)
XLA Ops:
  7.2 0.7 all-gather.2.cloned.1.call-update
  7.9 0.9 convert_reduce_fusion
  8.8 0.1 reduce_sum.58
  8.9 0.1 reduce_sum.61
  9.0 0.1 reduce_sum.59
  9.1 0.1 reduce_sum.62
  9.2 23.3 %all-reduce.2 = (f32[16]{0:T(128)S(1)}, f32[16]{0:T(128)S(1)}) all-reduce(f32[16]{0:T(128)S(1)} %reduce_sum.62, f32[16]{0:T(128)S(1)} %reduce_sum.59), channel_id=1, replica_groups=mesh['groups'=2,'space'=4,'tm'=2,'chan'=2] {'space','tm'}, use_global_device_ids=true, to_apply=%region_5.0 | all-reduce | flops 32 | bytes 256 | tf_op jit(solution)/shard_map/psum | solution.py:39
  32.6 0.1 mul.77
  32.8 0.1 sub.43
  32.9 0.9 fusion.26
  33.7 3.8 %all_to_all.35 = bf16[2,64,256]{2,1,0:T(8,128)(2,1)S(1)} all-to-all(bf16[2,64,256]{2,1,0:T(8,128)(2,1)S(1)} %fusion.26), channel_id=1, replica_groups=mesh['groups'=2,'space'=4,'tm'=2,'chan'=2] {'chan'}, dimensions={0} | all-to-all | bytes 131072 | tf_op jit(solution)/shard_map/all_to_all | solution.py:53
  37.5 0.2 convolution_convert_fusion.2
  37.8 14.3 %all_gather.12 = bf16[256,512]{1,0:T(8,128)(2,1)S(1)} all-gather(bf16[64,512]{1,0:T(8,128)(2,1)S(1)} %convolution_convert_fusion.2), channel_id=1, replica_groups=mesh['groups'=2,'space'=4,'tm'=2,'chan'=2] {'space'}, dimensions={0}, use_global_device_ids=true | all-gather | bytes 327680 | tf_op jit(solution)/shard_map/all_gather | solution.py:60
  52.1 1.2 convolution_convert_fusion.1
  53.3 13.9 %all_gather.13 = bf16[256,512]{1,0:T(8,128)(2,1)S(1)} all-gather(bf16[64,512]{1,0:T(8,128)(2,1)S(1)} %convolution_convert_fusion.1), channel_id=1, replica_groups=mesh['groups'=2,'space'=4,'tm'=2,'chan'=2] {'space'}, dimensions={0}, use_global_device_ids=true | all-gather | bytes 327680 | tf_op jit(solution)/shard_map/all_gather | solution.py:61
  67.2 1.5 %fusion.37 = (f32[64]{0:T(128)S(1)}, f32[64,256]{1,0:T(8,128)S(1)}) fusion(bf16[256,512]{1,0:T(8,128)(2,1)S(1)} %all_gather.12, bf16[64,512]{1,0:T(8,128)(2,1)S(1)} %bitcast.164, bf16[512,512]{1,0:T(8,128)(2,1)} %param.11), kind=kOutput, calls=%fused_computation.104 | convolution fusion | flops 50397120 | bytes 917760 | tf_op jit(solution)/shard_map/dot_general | solution.py:62
  68.7 0.2 fusion.28
  68.9 1.4 convolution_convert_fusion
  70.3 3.8 %all_to_all.36 = bf16[64,2,256]{2,0,1:T(8,128)(2,1)S(1)} all-to-all(bf16[64,2,256]{2,0,1:T(8,128)(2,1)S(1)} %bitcast.193), channel_id=1, replica_groups=mesh['groups'=2,'space'=4,'tm'=2,'chan'=2] {'chan'}, dimensions={1} | all-to-all | bytes 131072 | tf_op jit(solution)/shard_map/all_to_all | solution.py:71
  74.2 0.1 reduce_sum.81
  74.3 0.1 reduce_sum.82
  74.5 0.1 reduce_sum.85
  74.6 17.4 %all-reduce.1 = (f32[16]{0:T(128)S(1)}, f32[16]{0:T(128)S(1)}) all-reduce(f32[16]{0:T(128)S(1)} %reduce_sum.85, f32[16]{0:T(128)S(1)} %reduce_sum.82), channel_id=1, replica_groups=mesh['groups'=2,'space'=4,'tm'=2,'chan'=2] {'space','tm'}, use_global_device_ids=true, to_apply=%region_13.14 | all-reduce | flops 32 | bytes 256 | tf_op jit(solution)/shard_map/psum | solution.py:39
  92.1 0.1 mul.87
  92.3 0.1 sub.50
  92.4 1.9 %all_gather.14 = bf16[2,1,64,512]{3,2,1,0:T(8,128)(2,1)S(1)} all-gather(bf16[2,1,64,256]{3,2,1,0:T(8,128)(2,1)S(1)} %multiply_convert_fusion), channel_id=1, replica_groups=mesh['groups'=2,'space'=4,'tm'=2,'chan'=2] {'chan'}, dimensions={3}, use_global_device_ids=true | all-gather | bytes 196608 | tf_op jit(solution)/shard_map/all_gather | solution.py:76
  94.3 4.1 %collective-permute-start = (bf16[2,1,64,512]{3,2,1,0:T(8,128)(2,1)S(1)}, bf16[2,1,64,512]{3,2,1,0:T(8,128)(2,1)S(1)}, u32[]{:S(2)}, u32[]{:S(2)}) collective-permute-start(bf16[2,1,64,512]{3,2,1,0:T(8,128)(2,1)S(1)} %all_gather.14), channel_id=1, source_target_pairs={{0,2},{1,3},{4,6},{5,7},{8,10},{9,11},{12,14},{13,15},{16,18},{17,... | collective-permute-start | bytes 393224 | tf_op jit(solution)/shard_map/ppermute | solution.py:14
  98.4 4.3 %collective-permute-done = bf16[2,1,64,512]{3,2,1,0:T(8,128)(2,1)S(1)} collective-permute-done((bf16[2,1,64,512]{3,2,1,0:T(8,128)(2,1)S(1)}, bf16[2,1,64,512]{3,2,1,0:T(8,128)(2,1)S(1)}, u32[]{:S(2)}, u32[]{:S(2)}) %collective-permute-start) | collective-permute-done | bytes 131104 | tf_op jit(solution)/shard_map/ppermute | solution.py:14
  102.8 3.0 %collective-permute-start.1 = (bf16[4,1,64,512]{3,2,1,0:T(8,128)(2,1)S(1)}, bf16[4,1,64,512]{3,2,1,0:T(8,128)(2,1)S(1)}, u32[]{:S(2)}, u32[]{:S(2)}) collective-permute-start(bf16[4,1,64,512]{3,2,1,0:T(8,128)(2,1)S(1)} %constant_dynamic-update-slice_fusion), channel_id=1, source_target_pairs={{0,4},{4,8},{8,12},{1,5},{5,9},{9,13},{2,6},{6,10},{10,14},{3,7},{... | collective-permute-start | bytes 786440 | tf_op jit(solution)/shard_map/ppermute | solution.py:25
  105.8 1.3 collective-permute-start.2
  107.1 3.8 %collective-permute-done.1 = bf16[4,1,64,512]{3,2,1,0:T(8,128)(2,1)S(1)} collective-permute-done((bf16[4,1,64,512]{3,2,1,0:T(8,128)(2,1)S(1)}, bf16[4,1,64,512]{3,2,1,0:T(8,128)(2,1)S(1)}, u32[]{:S(2)}, u32[]{:S(2)}) %collective-permute-start.1) | collective-permute-done | bytes 262176 | tf_op jit(solution)/shard_map/ppermute | solution.py:25
  110.9 4.1 %collective-permute-done.2 = bf16[4,1,64,512]{3,2,1,0:T(8,128)(2,1)S(1)} collective-permute-done((bf16[4,1,64,512]{3,2,1,0:T(8,128)(2,1)S(1)}, bf16[4,1,64,512]{3,2,1,0:T(8,128)(2,1)S(1)}, u32[]{:S(2)}, u32[]{:S(2)}) %collective-permute-start.2) | collective-permute-done | bytes 262176 | tf_op jit(solution)/shard_map/ppermute | solution.py:27
  115.0 0.2 fusion.13
  115.3 0.7 fusion.36
  116.0 0.8 fusion.35
  116.8 0.4 fusion.34
  117.2 1.3 fusion.20
  118.5 1.7 %fusion.19 = f32[128,256]{1,0:T(8,128)S(1)} fusion(bf16[128,512]{1,0:T(8,128)(2,1)S(1)} %bitcast.184, bf16[3,3,3,512,256]{4,3,2,1,0:T(8,128)(2,1)} %all-gather.2.cloned.1.call-done), kind=kOutput, calls=%fused_computation.69 | convolution fusion | flops 33554432 | bytes 524288 | tf_op jit(solution)/shard_map/dot_general | solution.py:102
  120.2 1.1 fusion.18
  121.4 1.1 fusion.17
  122.5 1.1 fusion.16
  123.7 1.2 fusion.15
  124.8 1.1 fusion.14
  126.0 1.1 convolution_add_fusion.19
  127.1 1.1 convolution_add_fusion.18
  128.3 1.1 convolution_add_fusion.17
  129.4 1.1 fusion.6
  130.6 1.1 convolution_add_fusion.15
  131.7 1.1 fusion.5
  132.8 0.2 convolution_add_fusion.13
  133.0 0.2 fusion.4
  133.2 0.2 convolution_add_fusion.11
  133.4 0.2 convolution_add_fusion.10
  133.6 0.2 convolution_add_fusion.9
  133.8 0.2 convolution_add_fusion.8
  134.0 0.2 fusion.3
  134.2 0.2 convolution_add_fusion.6
  134.4 0.2 fusion.2
  134.6 0.2 convolution_add_fusion.4
  134.8 0.2 convolution_add_fusion.3
  135.0 0.2 convolution_add_fusion.2
  135.2 0.2 convolution_add_fusion.1
  135.4 0.8 fusion.8
  136.3 0.6 copy.24
  (33 shorter events, 0.6 us)
Async XLA Ops:
  7.2 30.4 %copy-start = (bf16[512,512]{1,0:T(8,128)(2,1)S(1)}, bf16[512,512]{1,0:T(8,128)(2,1)}, u32[]{:S(2)}) copy-start(bf16[512,512]{1,0:T(8,128)(2,1)} %param.12) | copy-start | bytes 1572868
  7.2 67.0 %copy-start.2 = (bf16[2,1,64,256]{3,2,1,0:T(8,128)(2,1)S(1)}, bf16[2,1,64,256]{3,2,1,0:T(8,128)(2,1)}, u32[]{:S(2)}) copy-start(bf16[2,1,64,256]{3,2,1,0:T(8,128)(2,1)} %param.8) | copy-start | bytes 196612
  7.2 85.1 %copy-start.7 = (f32[256]{0:T(256)S(1)}, f32[256]{0:T(256)}, u32[]{:S(2)}) copy-start(f32[256]{0:T(256)} %param.10) | copy-start | bytes 3076
  7.2 110.0 %all-gather.2.cloned.1.call-start = ((), (), s32[]{:S(2)}) async-start(), calls=%async_computation.2 | async-start | bytes 10616832 | tf_op jit(solution)/shard_map/all_gather | solution.py:92
  94.3 8.4 %collective-permute-start = (bf16[2,1,64,512]{3,2,1,0:T(8,128)(2,1)S(1)}, bf16[2,1,64,512]{3,2,1,0:T(8,128)(2,1)S(1)}, u32[]{:S(2)}, u32[]{:S(2)}) collective-permute-start(bf16[2,1,64,512]{3,2,1,0:T(8,128)(2,1)S(1)} %all_gather.14), channel_id=1, source_target_pairs={{0,2},{1,3},{4,6},{5,7},{8,10},{9,11},{12,14},{13,15},{16,18},{17,... | collective-permute-start | bytes 393224 | tf_op jit(solution)/shard_map/ppermute | solution.py:14
  102.8 8.1 %collective-permute-start.1 = (bf16[4,1,64,512]{3,2,1,0:T(8,128)(2,1)S(1)}, bf16[4,1,64,512]{3,2,1,0:T(8,128)(2,1)S(1)}, u32[]{:S(2)}, u32[]{:S(2)}) collective-permute-start(bf16[4,1,64,512]{3,2,1,0:T(8,128)(2,1)S(1)} %constant_dynamic-update-slice_fusion), channel_id=1, source_target_pairs={{0,4},{4,8},{8,12},{1,5},{5,9},{9,13},{2,6},{6,10},{10,14},{3,7},{... | collective-permute-start | bytes 786440 | tf_op jit(solution)/shard_map/ppermute | solution.py:25
  105.8 9.2 %collective-permute-start.2 = (bf16[4,1,64,512]{3,2,1,0:T(8,128)(2,1)S(1)}, bf16[4,1,64,512]{3,2,1,0:T(8,128)(2,1)S(1)}, u32[]{:S(2)}, u32[]{:S(2)}) collective-permute-start(bf16[4,1,64,512]{3,2,1,0:T(8,128)(2,1)S(1)} %constant_dynamic-update-slice_fusion), channel_id=1, source_target_pairs={{4,0},{8,4},{12,8},{5,1},{9,5},{13,9},{6,2},{10,6},{14,10},{7,3},{... | collective-permute-start | bytes 786440 | tf_op jit(solution)/shard_map/ppermute | solution.py:27
  117.2 14.5 %copy-start.1 = (bf16[3,3,3,512,256]{4,3,2,1,0:T(8,128)(2,1)S(1)}, bf16[3,3,3,512,256]{4,3,2,1,0:T(8,128)(2,1)}, u32[]{:S(2)}) copy-start(bf16[3,3,3,512,256]{4,3,2,1,0:T(8,128)(2,1)} %all-gather.2.cloned.1.call-done) | copy-start | bytes 21233668
  117.2 15.8 %copy-start.6 = (bf16[2,1,64,512]{3,2,1,0:T(8,128)(2,1)S(1)}, bf16[2,1,64,512]{3,2,1,0:T(8,128)(2,1)}, u32[]{:S(2)}) copy-start(bf16[2,1,64,512]{3,2,1,0:T(8,128)(2,1)} %get-tuple-element.38) | copy-start | bytes 393220
  117.2 16.8 %copy-start.5 = (bf16[2,1,64,512]{3,2,1,0:T(8,128)(2,1)S(1)}, bf16[2,1,64,512]{3,2,1,0:T(8,128)(2,1)}, u32[]{:S(2)}) copy-start(bf16[2,1,64,512]{3,2,1,0:T(8,128)(2,1)} %get-tuple-element.35) | copy-start | bytes 393220
  117.2 17.2 %copy-start.4 = (bf16[2,1,64,512]{3,2,1,0:T(8,128)(2,1)S(1)}, bf16[2,1,64,512]{3,2,1,0:T(8,128)(2,1)}, u32[]{:S(2)}) copy-start(bf16[2,1,64,512]{3,2,1,0:T(8,128)(2,1)} %get-tuple-element.37) | copy-start | bytes 393220
  123.6 11.8 %copy-start.3 = (bf16[2,1,64,512]{3,2,1,0:T(8,128)(2,1)S(1)}, bf16[2,1,64,512]{3,2,1,0:T(8,128)(2,1)}, u32[]{:S(2)}) copy-start(bf16[2,1,64,512]{3,2,1,0:T(8,128)(2,1)} %get-tuple-element.34) | copy-start | bytes 393220
Sparse Core Ops, SparseCore 0:
  9.6 92.6 all-gather.1
where the time goes:
time: 145 us; the launch traced here: 144 us
  blocking collectives  78.5 us (54%)
  matrix products  23.1 us (16%)
  between operations  14.5 us (10%)
  waiting for transfers between devices  12.9 us (9%)
  starting transfers between devices  8.43 us (6%)
  local copies, waits for them, and re-layouts  3.52 us (2%)
  other arithmetic  2.8 us (2%)
    psum x2, blocking collectives, normalize(): lax.psum((jnp.sum(grouped, axis=(0, 2)), jnp.sum(grouped * grouped, axis=...  40.8 us
    dot_general x27, matrix products, convolve(): jnp.dot(window, piece[time_tap, row_tap, col_tap], preferred_element_type...  18.8 us
    all_gather x1, blocking collectives, attend(): key_piece = lax.all_gather(keyed, 'space', axis=0, tiled=True)  14.3 us
    all_gather x1, blocking collectives, attend(): value_piece = lax.all_gather(valued, 'space', axis=0, tiled=True)  13.9 us
    ppermute x1, waiting for transfers between devices, shifted_2(): return lax.ppermute(x, axis, pairs)  4.29 us
    ppermute x1, waiting for transfers between devices, padded_2(): lax.ppermute(head, axis, [((i + 1) % count, i) for i in range(ends)])  4.13 us
    ppermute x1, starting transfers between devices, shifted_2(): return lax.ppermute(x, axis, pairs)  4.12 us
    ppermute x1, waiting for transfers between devices, padded_2(): lax.ppermute(tail, axis, [(i, (i + 1) % count) for i in range(ends)])  3.8 us
  transfers between devices with their start and end apart: 4, of which 3 were waited for; matrix products, arithmetic and copies ran while one was open for 7% of the time, Pallas kernels for 0%

commit v1 on v0

--- a/solution.py
+++ b/solution.py
@@ -1,11 +1,22 @@
+import functools
 import jax
 import jax.numpy as jnp
 from jax import lax
 from jax.sharding import PartitionSpec as P
+from jax.lax import psum
 
 D = 512
 NGROUP = 32
 EPSILON = 1e-06
+
+
+def shape_space(message, axis_key, group_axis):
+    clean = psum(message, axis_key)
+    local_out = psum(clean, group_axis)
+    return local_out
+
+
+scan_roots_in = functools.partial(shape_space, axis_key="tm", group_axis="space")
 
 
 def shifted_2(x, axis, by):
@@ -36,8 +47,8 @@
     group_width = D // NGROUP
     grouped = source.reshape(-1, channels // group_width, group_width)
     population = grouped.shape[0] * group_width * lax.axis_size("space") * lax.axis_size("tm")
-    group_sums, group_squares = lax.psum(
-        (jnp.sum(grouped, axis=(0, 2)), jnp.sum(grouped * grouped, axis=(0, 2))), ("space", "tm")
+    group_sums, group_squares = scan_roots_in(
+        (jnp.sum(grouped, axis=(0, 2)), jnp.sum(grouped * grouped, axis=(0, 2)))
     )
     centre = group_sums / population
     spread = jnp.maximum(group_squares / population - centre * centre, 0.0)

time: 145 us -> 138 us (0.952)
  blocking collectives: 78.5 us -> 70.1 us
  waiting for transfers between devices: 12.9 us -> 15.1 us
    psum x2 -> x4, blocking collectives: 40.8 us -> 32.4 us  [the longest x2 21.4 us: shape_space(): local_out = psum(clean, group_axis)]
    ppermute x1, waiting for transfers between devices: 4.29 us -> 6.44 us  [shifted_2(): return lax.ppermute(x, axis, pairs)]
where the time goes in v1:
time: 138 us; the launch traced here: 137 us
  blocking collectives  70.1 us (51%)
  matrix products  23.1 us (17%)
  waiting for transfers between devices  15.1 us (11%)
  between operations  14.5 us (11%)
  starting transfers between devices  8.07 us (6%)
  local copies, waits for them, and re-layouts  3.52 us (3%)
  other arithmetic  2.81 us (2%)
    psum x2, blocking collectives, shape_space(): local_out = psum(clean, group_axis)  21.4 us
    dot_general x27, matrix products, convolve(): jnp.dot(window, piece[time_tap, row_tap, col_tap], preferred_element_type...  18.8 us
    all_gather x1, blocking collectives, attend(): key_piece = lax.all_gather(keyed, 'space', axis=0, tiled=True)  14.3 us
    all_gather x1, blocking collectives, attend(): value_piece = lax.all_gather(valued, 'space', axis=0, tiled=True)  13.9 us
    psum x2, blocking collectives, shape_space(): clean = psum(message, axis_key)  11 us
    ppermute x1, waiting for transfers between devices, shifted_2(): return lax.ppermute(x, axis, pairs)  6.44 us
    ppermute x1, waiting for transfers between devices, padded_2(): lax.ppermute(head, axis, [((i + 1) % count, i) for i in range(ends)])  4.13 us
    ppermute x1, waiting for transfers between devices, padded_2(): lax.ppermute(tail, axis, [(i, (i + 1) % count) for i in range(ends)])  3.8 us
  transfers between devices with their start and end apart: 4, of which 3 were waited for; matrix products, arithmetic and copies ran while one was open for 7% of the time, Pallas kernels for 0%

profile of v1, /device:TPU:0, one launch (start us, length us, event | category | flops | bytes accessed | tf_op | source)
XLA Modules:
  0.0 137.2 jit_solution(8726998503000692527)
XLA Ops:
  7.2 0.7 all-gather.2.cloned.1.call-update
  7.9 0.9 convert_reduce_fusion
  9.0 0.1 reduce_sum.59
  9.1 0.1 reduce_sum.62
  9.2 5.9 %all-reduce.4 = (f32[16]{0:T(128)S(1)}, f32[16]{0:T(128)S(1)}) all-reduce(f32[16]{0:T(128)S(1)} %reduce_sum.62, f32[16]{0:T(128)S(1)} %reduce_sum.59), channel_id=1, replica_groups=mesh['groups'=2,'space'=4,'tm'=2,'chan'=2] {'tm'}, use_global_device_ids=true, to_apply=%region_6.0 | all-reduce | flops 32 | bytes 256 | tf_op jit(solution)/shard_map/psum | solution.py:14
  15.1 12.5 %all-reduce.2 = (f32[16]{0:T(128)S(1)}, f32[16]{0:T(128)S(1)}) all-reduce(f32[16]{0:T(128)S(1)} %get-tuple-element.18, f32[16]{0:T(128)S(1)} %get-tuple-element.19), channel_id=1, replica_groups=mesh['groups'=2,'space'=4,'tm'=2,'chan'=2] {'space'}, use_global_device_ids=true, to_apply=%region_7.0 | all-reduce | flops 32 | bytes 256 | tf_op jit(solution)/shard_map/psum | solution.py:15
  27.6 0.1 mul.77
  27.8 0.1 sub.43
  27.9 0.9 fusion.26
  28.8 3.8 %all_to_all.35 = bf16[2,64,256]{2,1,0:T(8,128)(2,1)S(1)} all-to-all(bf16[2,64,256]{2,1,0:T(8,128)(2,1)S(1)} %fusion.26), channel_id=1, replica_groups=mesh['groups'=2,'space'=4,'tm'=2,'chan'=2] {'chan'}, dimensions={0} | all-to-all | bytes 131072 | tf_op jit(solution)/shard_map/all_to_all | solution.py:64
  32.6 0.2 convolution_convert_fusion.2
  32.8 14.3 %all_gather.12 = bf16[256,512]{1,0:T(8,128)(2,1)S(1)} all-gather(bf16[64,512]{1,0:T(8,128)(2,1)S(1)} %convolution_convert_fusion.2), channel_id=1, replica_groups=mesh['groups'=2,'space'=4,'tm'=2,'chan'=2] {'space'}, dimensions={0}, use_global_device_ids=true | all-gather | bytes 327680 | tf_op jit(solution)/shard_map/all_gather | solution.py:71
  47.1 1.2 convolution_convert_fusion.1
  48.3 13.9 %all_gather.13 = bf16[256,512]{1,0:T(8,128)(2,1)S(1)} all-gather(bf16[64,512]{1,0:T(8,128)(2,1)S(1)} %convolution_convert_fusion.1), channel_id=1, replica_groups=mesh['groups'=2,'space'=4,'tm'=2,'chan'=2] {'space'}, dimensions={0}, use_global_device_ids=true | all-gather | bytes 327680 | tf_op jit(solution)/shard_map/all_gather | solution.py:72
  62.2 1.5 %fusion.37 = (f32[64]{0:T(128)S(1)}, f32[64,256]{1,0:T(8,128)S(1)}) fusion(bf16[256,512]{1,0:T(8,128)(2,1)S(1)} %all_gather.12, bf16[64,512]{1,0:T(8,128)(2,1)S(1)} %bitcast.164, bf16[512,512]{1,0:T(8,128)(2,1)} %param.11), kind=kOutput, calls=%fused_computation.104 | convolution fusion | flops 50397120 | bytes 917760 | tf_op jit(solution)/shard_map/dot_general | solution.py:73
  63.7 0.2 fusion.28
  63.9 1.4 %convolution_convert_fusion = bf16[64,512]{1,0:T(8,128)(2,1)S(1)} fusion(bf16[512,512]{1,0:T(8,128)(2,1)} %param.14, bf16[256,512]{1,0:T(8,128)(2,1)S(1)} %all_gather.13, f32[64]{0:T(128)S(1)} %fusion.28, f32[64,256]{1,0:T(8,128)S(1)} %get-tuple-element.49, f32[64]{0:T(128)S(1)} %broadcast_maximum_fusion), kind=kOutput, calls=%fused_computation.32 | convolution fusion | flops 50462720 | bytes 918016 | tf_op jit(solution)/shard_map/dot_general | solution.py:81
  65.4 3.8 %all_to_all.36 = bf16[64,2,256]{2,0,1:T(8,128)(2,1)S(1)} all-to-all(bf16[64,2,256]{2,0,1:T(8,128)(2,1)S(1)} %bitcast.193), channel_id=1, replica_groups=mesh['groups'=2,'space'=4,'tm'=2,'chan'=2] {'chan'}, dimensions={1} | all-to-all | bytes 131072 | tf_op jit(solution)/shard_map/all_to_all | solution.py:82
  69.2 0.1 reduce_sum.81
  69.3 0.1 reduce_sum.82
  69.5 0.1 reduce_sum.85
  69.6 5.1 %all-reduce.3 = (f32[16]{0:T(128)S(1)}, f32[16]{0:T(128)S(1)}) all-reduce(f32[16]{0:T(128)S(1)} %reduce_sum.85, f32[16]{0:T(128)S(1)} %reduce_sum.82), channel_id=1, replica_groups=mesh['groups'=2,'space'=4,'tm'=2,'chan'=2] {'tm'}, use_global_device_ids=true, to_apply=%region_16.17 | all-reduce | flops 32 | bytes 256 | tf_op jit(solution)/shard_map/psum | solution.py:14
  74.7 8.9 %all-reduce.1 = (f32[16]{0:T(128)S(1)}, f32[16]{0:T(128)S(1)}) all-reduce(f32[16]{0:T(128)S(1)} %get-tuple-element.16, f32[16]{0:T(128)S(1)} %get-tuple-element.17), channel_id=1, replica_groups=mesh['groups'=2,'space'=4,'tm'=2,'chan'=2] {'space'}, use_global_device_ids=true, to_apply=%region_17.18 | all-reduce | flops 32 | bytes 256 | tf_op jit(solution)/shard_map/psum | solution.py:15
  83.7 0.1 mul.87
  83.9 0.1 sub.50
  84.0 1.9 %all_gather.14 = bf16[2,1,64,512]{3,2,1,0:T(8,128)(2,1)S(1)} all-gather(bf16[2,1,64,256]{3,2,1,0:T(8,128)(2,1)S(1)} %multiply_convert_fusion), channel_id=1, replica_groups=mesh['groups'=2,'space'=4,'tm'=2,'chan'=2] {'chan'}, dimensions={3}, use_global_device_ids=true | all-gather | bytes 196608 | tf_op jit(solution)/shard_map/all_gather | solution.py:87
  85.9 3.4 %collective-permute-start = (bf16[2,1,64,512]{3,2,1,0:T(8,128)(2,1)S(1)}, bf16[2,1,64,512]{3,2,1,0:T(8,128)(2,1)S(1)}, u32[]{:S(2)}, u32[]{:S(2)}) collective-permute-start(bf16[2,1,64,512]{3,2,1,0:T(8,128)(2,1)S(1)} %all_gather.14), channel_id=1, source_target_pairs={{0,2},{1,3},{4,6},{5,7},{8,10},{9,11},{12,14},{13,15},{16,18},{17,... | collective-permute-start | bytes 393224 | tf_op jit(solution)/shard_map/ppermute | solution.py:25
  89.3 6.4 %collective-permute-done = bf16[2,1,64,512]{3,2,1,0:T(8,128)(2,1)S(1)} collective-permute-done((bf16[2,1,64,512]{3,2,1,0:T(8,128)(2,1)S(1)}, bf16[2,1,64,512]{3,2,1,0:T(8,128)(2,1)S(1)}, u32[]{:S(2)}, u32[]{:S(2)}) %collective-permute-start) | collective-permute-done | bytes 131104 | tf_op jit(solution)/shard_map/ppermute | solution.py:25
  95.8 3.3 %collective-permute-start.1 = (bf16[4,1,64,512]{3,2,1,0:T(8,128)(2,1)S(1)}, bf16[4,1,64,512]{3,2,1,0:T(8,128)(2,1)S(1)}, u32[]{:S(2)}, u32[]{:S(2)}) collective-permute-start(bf16[4,1,64,512]{3,2,1,0:T(8,128)(2,1)S(1)} %constant_dynamic-update-slice_fusion), channel_id=1, source_target_pairs={{0,4},{4,8},{8,12},{1,5},{5,9},{9,13},{2,6},{6,10},{10,14},{3,7},{... | collective-permute-start | bytes 786440 | tf_op jit(solution)/shard_map/ppermute | solution.py:36
  99.2 1.3 collective-permute-start.2
  100.5 3.8 %collective-permute-done.1 = bf16[4,1,64,512]{3,2,1,0:T(8,128)(2,1)S(1)} collective-permute-done((bf16[4,1,64,512]{3,2,1,0:T(8,128)(2,1)S(1)}, bf16[4,1,64,512]{3,2,1,0:T(8,128)(2,1)S(1)}, u32[]{:S(2)}, u32[]{:S(2)}) %collective-permute-start.1) | collective-permute-done | bytes 262176 | tf_op jit(solution)/shard_map/ppermute | solution.py:36
  104.3 4.1 %collective-permute-done.2 = bf16[4,1,64,512]{3,2,1,0:T(8,128)(2,1)S(1)} collective-permute-done((bf16[4,1,64,512]{3,2,1,0:T(8,128)(2,1)S(1)}, bf16[4,1,64,512]{3,2,1,0:T(8,128)(2,1)S(1)}, u32[]{:S(2)}, u32[]{:S(2)}) %collective-permute-start.2) | collective-permute-done | bytes 262176 | tf_op jit(solution)/shard_map/ppermute | solution.py:38
  108.4 0.2 fusion.13
  108.7 0.7 fusion.36
  109.4 0.8 fusion.35
  110.2 0.4 fusion.34
  110.6 1.3 fusion.20
  111.9 1.7 %fusion.19 = f32[128,256]{1,0:T(8,128)S(1)} fusion(bf16[128,512]{1,0:T(8,128)(2,1)S(1)} %bitcast.184, bf16[3,3,3,512,256]{4,3,2,1,0:T(8,128)(2,1)} %all-gather.2.cloned.1.call-done), kind=kOutput, calls=%fused_computation.69 | convolution fusion | flops 33554432 | bytes 524288 | tf_op jit(solution)/shard_map/dot_general | solution.py:113
  113.6 1.1 fusion.18
  114.8 1.1 fusion.17
  115.9 1.1 fusion.16
  117.1 1.2 fusion.15
  118.2 1.1 fusion.14
  119.4 1.1 convolution_add_fusion.19
  120.5 1.1 convolution_add_fusion.18
  121.7 1.1 convolution_add_fusion.17
  122.8 1.1 fusion.6
  124.0 1.1 convolution_add_fusion.15
  125.1 1.1 fusion.5
  126.2 0.2 convolution_add_fusion.13
  126.4 0.2 fusion.4
  126.6 0.2 convolution_add_fusion.11
  126.8 0.2 convolution_add_fusion.10
  127.0 0.2 convolution_add_fusion.9
  127.2 0.2 convolution_add_fusion.8
  127.4 0.2 fusion.3
  127.6 0.2 convolution_add_fusion.6
  127.9 0.2 fusion.2
  128.1 0.2 convolution_add_fusion.4
  128.3 0.2 convolution_add_fusion.3
  128.4 0.2 convolution_add_fusion.2
  128.6 0.2 convolution_add_fusion.1
  128.9 0.8 fusion.8
  129.7 0.6 copy.24
  (35 shorter events, 0.8 us)
Async XLA Ops:
  7.2 25.4 %copy-start = (bf16[512,512]{1,0:T(8,128)(2,1)S(1)}, bf16[512,512]{1,0:T(8,128)(2,1)}, u32[]{:S(2)}) copy-start(bf16[512,512]{1,0:T(8,128)(2,1)} %param.12) | copy-start | bytes 1572868
  7.2 62.0 %copy-start.2 = (bf16[2,1,64,256]{3,2,1,0:T(8,128)(2,1)S(1)}, bf16[2,1,64,256]{3,2,1,0:T(8,128)(2,1)}, u32[]{:S(2)}) copy-start(bf16[2,1,64,256]{3,2,1,0:T(8,128)(2,1)} %param.8) | copy-start | bytes 196612
  7.2 76.8 %copy-start.7 = (f32[256]{0:T(256)S(1)}, f32[256]{0:T(256)}, u32[]{:S(2)}) copy-start(f32[256]{0:T(256)} %param.10) | copy-start | bytes 3076
  7.2 103.4 %all-gather.2.cloned.1.call-start = ((), (), s32[]{:S(2)}) async-start(), calls=%async_computation.2 | async-start | bytes 10616832 | tf_op jit(solution)/shard_map/all_gather | solution.py:103
  85.9 9.9 %collective-permute-start = (bf16[2,1,64,512]{3,2,1,0:T(8,128)(2,1)S(1)}, bf16[2,1,64,512]{3,2,1,0:T(8,128)(2,1)S(1)}, u32[]{:S(2)}, u32[]{:S(2)}) collective-permute-start(bf16[2,1,64,512]{3,2,1,0:T(8,128)(2,1)S(1)} %all_gather.14), channel_id=1, source_target_pairs={{0,2},{1,3},{4,6},{5,7},{8,10},{9,11},{12,14},{13,15},{16,18},{17,... | collective-permute-start | bytes 393224 | tf_op jit(solution)/shard_map/ppermute | solution.py:25
  95.8 8.5 %collective-permute-start.1 = (bf16[4,1,64,512]{3,2,1,0:T(8,128)(2,1)S(1)}, bf16[4,1,64,512]{3,2,1,0:T(8,128)(2,1)S(1)}, u32[]{:S(2)}, u32[]{:S(2)}) collective-permute-start(bf16[4,1,64,512]{3,2,1,0:T(8,128)(2,1)S(1)} %constant_dynamic-update-slice_fusion), channel_id=1, source_target_pairs={{0,4},{4,8},{8,12},{1,5},{5,9},{9,13},{2,6},{6,10},{10,14},{3,7},{... | collective-permute-start | bytes 786440 | tf_op jit(solution)/shard_map/ppermute | solution.py:36
  99.2 9.2 %collective-permute-start.2 = (bf16[4,1,64,512]{3,2,1,0:T(8,128)(2,1)S(1)}, bf16[4,1,64,512]{3,2,1,0:T(8,128)(2,1)S(1)}, u32[]{:S(2)}, u32[]{:S(2)}) collective-permute-start(bf16[4,1,64,512]{3,2,1,0:T(8,128)(2,1)S(1)} %constant_dynamic-update-slice_fusion), channel_id=1, source_target_pairs={{4,0},{8,4},{12,8},{5,1},{9,5},{13,9},{6,2},{10,6},{14,10},{7,3},{... | collective-permute-start | bytes 786440 | tf_op jit(solution)/shard_map/ppermute | solution.py:38
  110.6 14.5 %copy-start.1 = (bf16[3,3,3,512,256]{4,3,2,1,0:T(8,128)(2,1)S(1)}, bf16[3,3,3,512,256]{4,3,2,1,0:T(8,128)(2,1)}, u32[]{:S(2)}) copy-start(bf16[3,3,3,512,256]{4,3,2,1,0:T(8,128)(2,1)} %all-gather.2.cloned.1.call-done) | copy-start | bytes 21233668
  110.6 15.8 %copy-start.6 = (bf16[2,1,64,512]{3,2,1,0:T(8,128)(2,1)S(1)}, bf16[2,1,64,512]{3,2,1,0:T(8,128)(2,1)}, u32[]{:S(2)}) copy-start(bf16[2,1,64,512]{3,2,1,0:T(8,128)(2,1)} %get-tuple-element.42) | copy-start | bytes 393220
  110.6 16.8 %copy-start.5 = (bf16[2,1,64,512]{3,2,1,0:T(8,128)(2,1)S(1)}, bf16[2,1,64,512]{3,2,1,0:T(8,128)(2,1)}, u32[]{:S(2)}) copy-start(bf16[2,1,64,512]{3,2,1,0:T(8,128)(2,1)} %get-tuple-element.39) | copy-start | bytes 393220
  110.6 17.2 %copy-start.4 = (bf16[2,1,64,512]{3,2,1,0:T(8,128)(2,1)S(1)}, bf16[2,1,64,512]{3,2,1,0:T(8,128)(2,1)}, u32[]{:S(2)}) copy-start(bf16[2,1,64,512]{3,2,1,0:T(8,128)(2,1)} %get-tuple-element.41) | copy-start | bytes 393220
  117.1 11.8 %copy-start.3 = (bf16[2,1,64,512]{3,2,1,0:T(8,128)(2,1)S(1)}, bf16[2,1,64,512]{3,2,1,0:T(8,128)(2,1)}, u32[]{:S(2)}) copy-start(bf16[2,1,64,512]{3,2,1,0:T(8,128)(2,1)} %get-tuple-element.38) | copy-start | bytes 393220
Sparse Core Ops, SparseCore 0:
  9.6 92.5 all-gather.1
